TPU v7x, 32 devices: a whole 2x2x4 slice. The times are simulated.
32 devices in a mesh: arc: 8 (over z, x), vec: 4 (over y, core).
Axes of the slice: x: 2, y: 2, z: 4, core: 2. Of those that a mesh axis runs over, the one named last changes fastest.
Arguments:
- right_side: float32 [640, 128, 128], P(('arc', 'vec')), may hold values from -6 to 6
- prior_diag: float32 [640, 128], P(('arc', 'vec')), may hold values from 0.5 to 4
- inv_factor: bfloat16 [512, 256, 256], P(('arc', 'vec'))
- coupling_panel: bfloat16 [512, 256, 1024], P(('arc', 'vec')), may hold values from -0.09375 to 0.09375
- coupling_owner: int32 [512, 8], replicated, may hold values from 0 to 31, all different within a row; in each aligned block of 16 rows (0 to 15, 16 to 31, ...) at most 5 rows name the same one
- coupling_block: int32 [512, 8], replicated, may hold values from 0 to 19
Outputs:
- solution_field: float32 [640, 128, 128], P(('arc', 'vec'))
- residual: float32 [640, 128, 128], P(('arc', 'vec'))
Inputs may be any that keep to these rules, and one draw needn't show every extreme that they name: `coupling_owner`: the 8 holders named for one arc are different. Among the 16 arcs of one device (aligned blocks of rows) no holder is named more than 5 times; some holder is named exactly 5 times.
All inputs are finite; a program needn't handle non-finite values.
Results may differ from a plain program's by a relative error of at most 0.006.
The roundings to bfloat16 on the way count: a program that leaves them out, or rounds other values in their place, can miss the bound.
Values may be sent and summed in bfloat16 or wider, within the bound.
No kernel may reach another device: no remote copies, remote signals or barrier semaphores. Data moves between devices by JAX's collectives and lax.ppermute only.
A program may use at most 128 MiB of HBM per device.

v0:
```python
import jax
import jax.numpy as jnp
from jax import lax
from jax.sharding import PartitionSpec as P

ITERS = 2


def inner_gram(left, right):
    return jnp.einsum("grc,grd->cd", left, right, precision=lax.Precision.HIGHEST)


def combine_cols(field, weights):
    return jnp.einsum("grc,cd->grd", field, weights, precision=lax.Precision.HIGHEST)


def times_high(left, right):
    return jnp.dot(left, right, precision=lax.Precision.HIGHEST)


def trade_out(buffer):
    return lax.all_to_all(buffer, ("arc", "vec"), split_axis=0, concat_axis=0, tiled=True)


def trade_back(buffer):
    return lax.all_to_all(buffer, ("arc", "vec"), split_axis=0, concat_axis=0, tiled=True)


def per_device(right_side, prior_diag, inv_factor, coupling_panel, coupling_owner, coupling_block):
    device_count = lax.axis_size(("arc", "vec"))
    my_index = lax.axis_index(("arc", "vec"))
    arcs_here = coupling_panel.shape[0]
    links = coupling_owner.shape[1]
    blocks_here = right_side.shape[0]
    block_rows = right_side.shape[1]
    rhs_count = right_side.shape[2]
    entries = arcs_here * links
    slot_count = (entries + device_count - 1) // device_count + 1
    owner_all = coupling_owner.reshape(device_count, entries)
    block_all = coupling_block.reshape(device_count, entries)
    position = jnp.arange(entries, dtype=jnp.int32)
    earlier = (owner_all[:, :, None] == owner_all[:, None, :]) & (
        position[None, None, :] < position[None, :, None]
    )
    rank_all = jnp.sum(earlier.astype(jnp.int32), axis=2)
    owner_mine = lax.dynamic_index_in_dim(owner_all, my_index, 0, keepdims=False)
    rank_mine = lax.dynamic_index_in_dim(rank_all, my_index, 0, keepdims=False)
    slot_mine = owner_mine * slot_count + rank_mine
    slot_ids = jnp.arange(slot_count, dtype=jnp.int32)
    matches = (owner_all[:, None, :] == my_index) & (
        rank_all[:, None, :] == slot_ids[None, :, None]
    )
    filled = jnp.any(matches, axis=2).reshape(-1)
    source_block = jnp.sum(jnp.where(matches, block_all[:, None, :], 0), axis=2).reshape(-1)
    block_ids = jnp.arange(blocks_here, dtype=jnp.int32)
    selector = ((source_block[:, None] == block_ids[None, :]) & filled[:, None]).astype(
        jnp.bfloat16
    )
    solution_field = jnp.zeros_like(right_side)
    residual = right_side
    direction = right_side
    res_gram = lax.psum(inner_gram(residual, residual), ("arc", "vec"))
    for sweep_index in range(ITERS):
        local_rounded = direction.astype(jnp.bfloat16)
        outgoing = jnp.where(
            filled[:, None, None], local_rounded[source_block], jnp.zeros((), jnp.bfloat16)
        )
        arrived = trade_out(outgoing)
        fetched = arrived[slot_mine].reshape(arcs_here, links * block_rows, rhs_count)
        coupled = jnp.einsum(
            "apk,akc->apc", coupling_panel, fetched, preferred_element_type=jnp.float32
        ).astype(jnp.bfloat16)
        whitened = jnp.einsum(
            "apq,aqc->apc", inv_factor, coupled, preferred_element_type=jnp.float32
        ).astype(jnp.bfloat16)
        smoothed = jnp.einsum(
            "aqp,aqc->apc", inv_factor, whitened, preferred_element_type=jnp.float32
        ).astype(jnp.bfloat16)
        projected = jnp.einsum(
            "apk,apc->akc", coupling_panel, smoothed, preferred_element_type=jnp.float32
        ).astype(jnp.bfloat16)
        projected = projected.reshape(entries, block_rows, rhs_count)
        returning = (
            jnp.zeros((device_count * slot_count, block_rows, rhs_count), jnp.bfloat16)
            .at[slot_mine]
            .set(projected)
        )
        came_back = trade_back(returning)
        summed = jnp.einsum("sb,src->brc", selector, came_back, preferred_element_type=jnp.float32)
        image_vec = prior_diag[:, :, None] * direction + summed
        curv_gram, image_gram, cross_gram = lax.psum(
            (
                inner_gram(direction, image_vec),
                inner_gram(image_vec, image_vec),
                inner_gram(residual, image_vec),
            ),
            ("arc", "vec"),
        )
        factor_low = jnp.linalg.cholesky(curv_gram)
        step_mat = jax.scipy.linalg.cho_solve((factor_low, True), res_gram)
        solution_field = solution_field + combine_cols(direction, step_mat)
        residual = residual - combine_cols(image_vec, step_mat)
        if sweep_index + 1 < ITERS:
            new_gram = (
                res_gram - times_high(step_mat.T, cross_gram.T) - times_high(cross_gram, step_mat)
            )
            new_gram = new_gram + times_high(step_mat.T, times_high(image_gram, step_mat))
            beta_mat = jax.scipy.linalg.cho_solve((jnp.linalg.cholesky(res_gram), True), new_gram)
            direction = residual + combine_cols(direction, beta_mat)
            res_gram = new_gram
    return (solution_field, residual)


def solution(mesh):
    in_specs = (
        P(("arc", "vec"), None, None),
        P(("arc", "vec"), None),
        P(("arc", "vec"), None, None),
        P(("arc", "vec"), None, None),
        P(),
        P(),
    )
    out_specs = (P(("arc", "vec"), None, None), P(("arc", "vec"), None, None))
    return jax.shard_map(
        per_device, mesh=mesh, in_specs=in_specs, out_specs=out_specs, check_vma=False
    )
```

profile of v0, /device:TPU:1, one launch (start us, length us, event | category | flops | bytes accessed | tf_op | source)
XLA Modules:
  0.0 1014.8 jit_solution(7668285359423061608)
XLA Ops:
  15.8 8.8 gather_fusion
  24.6 5.3 broadcast_select_fusion.1
  29.9 7.1 all-to-all-start
  37.1 116.3 %all-to-all-done = bf16[160,128,128]{2,1,0:T(8,128)(2,1)} async-done(((bf16[160,128,128]{2,1,0:T(8,128)(2,1)}), bf16[160,128,128]{2,1,0:T(8,128)(2,1)}, u32[]{:S(2)}, u32[]{:S(2)}) %all-to-all-start) | async-done | bytes 5242912 | tf_op jit(solution)/shard_map/all_to_all | solution.py:22
  153.4 5.6 gather_fusion.1
  159.0 9.2 convolution_convert_fusion.4
  168.2 7.3 convert_bitcast_fusion.1
  175.4 6.4 copy.148
  181.8 3.7 broadcast.116.clone
  185.5 19.3 %scatter_fusion = bf16[160,128,128]{2,1,0:T(8,128)(2,1)} fusion(bf16[160,128,128]{2,1,0:T(8,128)(2,1)} %broadcast.116.clone, s32[128]{0:T(128)S(1)} %fusion.35, bf16[128,128,128]{2,1,0:T(8,128)(2,1)} %bitcast.113), kind=kCustom, calls=%fused_computation.4 | custom fusion | bytes 12583424 | tf_op jit(solution)/shard_map/scatter | solution.py:86
  204.8 6.1 all-to-all-start.1
  214.2 113.1 %all-to-all-done.1 = bf16[160,128,128]{2,1,0:T(8,128)(2,1)} async-done(((bf16[160,128,128]{2,1,0:T(8,128)(2,1)}), bf16[160,128,128]{2,1,0:T(8,128)(2,1)}, u32[]{:S(2)}, u32[]{:S(2)}) %all-to-all-start.1) | async-done | bytes 5242912 | tf_op jit(solution)/shard_map/all_to_all | solution.py:26
  327.3 5.4 fusion.2
  340.3 125.8 %all-reduce.6.cloned.1.call-done = (f32[128,128]{0,1:T(8,128)}, f32[128,128]{0,1:T(8,128)}, f32[128,128]{1,0:T(8,128)}) async-done(((f32[128,128]{0,1:T(8,128)}, f32[128,128]{0,1:T(8,128)}, f32[128,128]{1,0:T(8,128)}), (f32[128,128]{0,1:T(8,128)}, f32[128,128]{0,1:T(8,128)}, f32[128,128]{1,0:T(8,128)})) %all-reduce.6.cloned.1.call-update) | async-done | bytes 196624 | tf_op jit(solution)/shard_map/psum | solution.py:62
  469.6 12.5 %cholesky.59 = f32[128,128]{1,0:T(8,128)S(1)} custom-call(f32[128,128]{1,0:T(8,128)} %get-tuple-element.20), custom_call_target="Cholesky" | custom-call | tf_op jit(solution)/shard_map/jit(cholesky)/cholesky | solution.py:99
  484.1 10.6 %custom-call.9 = f32[1,128,128]{1,2,0:T(8,128)S(1)} custom-call(f32[1,128,128]{2,1,0:T(8,128)} %fusion.9), custom_call_target="InvertDiagBlocksLowerTriangular" | custom-call | tf_op jit(solution)/shard_map/jit(_cho_solve)/triangular_solve | solution.py:100
  497.9 3.8 convolution_subtract_fusion.1
  501.7 13.2 %cholesky.70 = f32[128,128]{1,0:T(8,128)} custom-call(f32[128,128]{1,0:T(8,128)} %get-tuple-element.19), custom_call_target="Cholesky" | custom-call | tf_op jit(solution)/shard_map/jit(cholesky)/cholesky | solution.py:108
  518.5 11.4 %custom-call.10 = f32[1,128,128]{1,2,0:T(8,128)} custom-call(f32[1,128,128]{2,1,0:T(8,128)} %fusion.10), custom_call_target="InvertDiagBlocksLowerTriangular" | custom-call | tf_op jit(solution)/shard_map/jit(_cho_solve)/triangular_solve | solution.py:108
  534.7 3.8 fusion.36
  538.4 8.9 gather_fusion.2
  550.3 121.7 %all_to_all.20 = bf16[160,128,128]{2,1,0:T(8,128)(2,1)} all-to-all(bf16[160,128,128]{2,1,0:T(8,128)(2,1)S(1)} %broadcast_select_fusion), channel_id=1, replica_groups=mesh['arc'=8,'vec'=4] {'arc','vec'}, dimensions={0} | all-to-all | bytes 10485760 | tf_op jit(solution)/shard_map/all_to_all | solution.py:22
  672.0 5.7 gather_fusion.3
  677.7 9.2 convolution_convert_fusion.1
  686.9 7.2 convert_bitcast_fusion
  694.1 6.5 copy.164
  704.2 19.5 %scatter_fusion.1 = bf16[160,128,128]{2,1,0:T(8,128)(2,1)} fusion(bf16[160,128,128]{2,1,0:T(8,128)(2,1)} %broadcast.116, s32[128]{0:T(128)} %copy-done.12, bf16[128,128,128]{2,1,0:T(8,128)(2,1)} %bitcast.112), kind=kCustom, calls=%fused_computation.5 | custom fusion | bytes 12583424 | tf_op jit(solution)/shard_map/scatter | solution.py:86
  723.7 119.8 %all_to_all.21 = bf16[160,128,128]{2,1,0:T(8,128)(2,1)S(1)} all-to-all(bf16[160,128,128]{2,1,0:T(8,128)(2,1)} %scatter_fusion.1), channel_id=1, replica_groups=mesh['arc'=8,'vec'=4] {'arc','vec'}, dimensions={0} | all-to-all | bytes 10485760 | tf_op jit(solution)/shard_map/all_to_all | solution.py:26
  853.5 118.8 %all-reduce.4.cloned.1.call-done = f32[128,128]{0,1:T(8,128)} async-done(((f32[128,128]{0,1:T(8,128)}), f32[128,128]{0,1:T(8,128)}) %all-reduce.4.cloned.1.call-update) | async-done | bytes 65552 | tf_op jit(solution)/shard_map/psum | solution.py:91
  974.0 11.7 %cholesky.81 = f32[128,128]{1,0:T(8,128)S(1)} custom-call(f32[128,128]{1,0:T(8,128)S(1)} %fusion.15), custom_call_target="Cholesky" | custom-call | tf_op jit(solution)/shard_map/jit(cholesky)/cholesky | solution.py:99
  987.1 10.0 custom-call.11
  997.6 4.7 convolution_subtract_fusion
  (85 shorter events, 61.5 us)
Async XLA Ops:
  7.2 151.8 %copy-start = (bf16[16,256,256]{2,1,0:T(8,128)(2,1)S(1)}, bf16[16,256,256]{2,1,0:T(8,128)(2,1)}, u32[]{:S(2)}) copy-start(bf16[16,256,256]{2,1,0:T(8,128)(2,1)} %param.11) | copy-start | bytes 6291460
  7.2 7.6 copy-start.1
  14.8 9.8 copy-start.11
  29.9 123.5 %all-to-all-start = ((bf16[160,128,128]{2,1,0:T(8,128)(2,1)}), bf16[160,128,128]{2,1,0:T(8,128)(2,1)}, u32[]{:S(2)}, u32[]{:S(2)}) async-start(bf16[160,128,128]{2,1,0:T(8,128)(2,1)} %broadcast_select_fusion.1), calls=%async_computation | async-start | bytes 10485760 | tf_op jit(solution)/shard_map/all_to_all | solution.py:22
  37.0 148.5 %copy-start.12 = (s32[128]{0:T(128)}, s32[128]{0:T(128)S(1)}, u32[]{:S(2)}) copy-start(s32[128]{0:T(128)S(1)} %fusion.35) | copy-start | bytes 1540
  37.1 121.9 %copy-start.13 = (s32[1024]{0:T(1024)}, s32[1024]{0:T(1024)S(1)}, u32[]{:S(2)}) copy-start(s32[1024]{0:T(1024)S(1)} %pad_clamp_fusion) | copy-start | bytes 12292
  204.8 122.5 %all-to-all-start.1 = ((bf16[160,128,128]{2,1,0:T(8,128)(2,1)}), bf16[160,128,128]{2,1,0:T(8,128)(2,1)}, u32[]{:S(2)}, u32[]{:S(2)}) async-start(bf16[160,128,128]{2,1,0:T(8,128)(2,1)} %scatter_fusion), calls=%async_computation.1 | async-start | bytes 10485760 | tf_op jit(solution)/shard_map/all_to_all | solution.py:26
  211.0 255.2 %all-reduce.6.cloned.1.call-start = ((), (), s32[]{:S(2)}) async-start(), calls=%async_computation.5 | async-start | bytes 393216 | tf_op jit(solution)/shard_map/psum | solution.py:62
  211.4 121.4 %copy-start.9 = (s32[160]{0:T(256)}, s32[160]{0:T(256)S(1)}, u32[]{:S(2)}) copy-start(s32[160]{0:T(256)S(1)} %eq.60) | copy-start | bytes 1924
  214.2 118.5 %copy-start.8 = (f32[20,128]{1,0:T(8,128)S(1)}, f32[20,128]{1,0:T(8,128)}, u32[]{:S(2)}) copy-start(f32[20,128]{1,0:T(8,128)} %param.10) | copy-start | bytes 30724
  332.7 3.6 copy-start.4
  339.8 632.4 %all-reduce.4.cloned.1.call-start = ((), (), s32[]{:S(2)}) async-start(), calls=%async_computation.4 | async-start | bytes 131072 | tf_op jit(solution)/shard_map/psum | solution.py:91
  497.9 33.1 %copy-start.7 = (f32[128,128]{0,1:T(8,128)S(1)}, f32[128,128]{0,1:T(8,128)}, u32[]{:S(2)}) copy-start(f32[128,128]{0,1:T(8,128)} %get-tuple-element.15) | copy-start | bytes 196612
  723.7 119.8 %copy-start.10 = (s32[160]{0:T(256)S(1)}, s32[160]{0:T(256)}, u32[]{:S(2)}) copy-start(s32[160]{0:T(256)} %copy-done.9) | copy-start | bytes 1924
  843.5 4.1 copy-start.2
  846.4 1.2 copy-start.5
  997.6 4.7 copy-start.3
  997.6 4.7 copy-start.6
Sparse Core Ops, SparseCore 0:
  340.0 126.1 all-reduce.5
  851.2 120.9 all-reduce.3
where the time goes:
time: 1030 us; the launch traced here: 1010 us
  waiting for transfers between devices  474 us (46%)
  blocking collectives  242 us (23%)
  local copies, waits for them, and re-layouts  101 us (10%)
  other arithmetic  89.7 us (9%)
  matrix products  80 us (8%)
  between operations  14.8 us (1%)
  starting transfers between devices  14.1 us (1%)
    psum x1, waiting for transfers between devices, per_device(): res_gram = lax.psum(inner_gram(residual, residual), ('arc', 'vec'))  126 us
    all_to_all x1, blocking collectives, trade_out(): lax.all_to_all(buffer, ('arc', 'vec'), split_axis=0, concat_axis=0, tiled...  122 us
    all_to_all x1, blocking collectives, trade_back(): lax.all_to_all(buffer, ('arc', 'vec'), split_axis=0, concat_axis=0, tiled...  120 us
    psum x1, waiting for transfers between devices, per_device(): lax.psum((inner_gram(direction, image_vec), inner_gram(image_vec, image_v...  119 us
    all_to_all x1, waiting for transfers between devices, trade_out(): lax.all_to_all(buffer, ('arc', 'vec'), split_axis=0, concat_axis=0, tiled...  116 us
    all_to_all x1, waiting for transfers between devices, trade_back(): lax.all_to_all(buffer, ('arc', 'vec'), split_axis=0, concat_axis=0, tiled...  113 us
    scatter x2, local copies, waits for them, and re-layouts, per_device(): returning = jnp.zeros((device_count * slot_count, block_rows, rhs_count),...  38.8 us
    another operation x6, other arithmetic, per_device(): factor_low = jnp.linalg.cholesky(curv_gram)  25.7 us
  transfers between devices with their start and end apart: 4, of which 4 were waited for; matrix products, arithmetic and copies ran while one was open for 1% of the time, Pallas kernels for 0%

commit v1 on v0

--- a/solution.py
+++ b/solution.py
@@ -59,7 +59,7 @@
     solution_field = jnp.zeros_like(right_side)
     residual = right_side
     direction = right_side
-    res_gram = lax.psum(inner_gram(residual, residual), ("arc", "vec"))
+    res_gram = jnp.sum(lax.all_gather(inner_gram(residual, residual), ("arc", "vec")), axis=0)
     for sweep_index in range(ITERS):
         local_rounded = direction.astype(jnp.bfloat16)
         outgoing = jnp.where(

time: 1030 us -> 999 us (0.970)
  waiting for transfers between devices: 474 us -> 455 us
    psum x1 -> x0, waiting for transfers between devices: 126 us -> none  [per_device(): res_gram = lax.psum(inner_gram(residual, residual), ('arc', 'vec'))]
    psum x1 -> x2, waiting for transfers between devices: 119 us -> 233 us  [per_device(): lax.psum((inner_gram(direction, image_vec), inner_gram(image_vec, image_v...]
    all_to_all x1, waiting for transfers between devices: 113 us -> 7.11 us  [trade_back(): lax.all_to_all(buffer, ('arc', 'vec'), split_axis=0, concat_axis=0, tiled...]
    all_gather x0 -> x1, waiting for transfers between devices: none -> 98.6 us  [per_device(): lax.all_gather(inner_gram(residual, residual), ('arc', 'vec'))]
  transfers between devices with their start and end apart: 4 -> 5, of which waited for: 4 -> 5; matrix products, arithmetic and copies ran while one was open for 1% -> 3% of each run, Pallas kernels for 0% -> 0%
where the time goes in v1:
time: 999 us; the launch traced here: 988 us
  waiting for transfers between devices  455 us (46%)
  blocking collectives  240 us (24%)
  local copies, waits for them, and re-layouts  101 us (10%)
  other arithmetic  89.5 us (9%)
  matrix products  74.1 us (7%)
  between operations  14.3 us (1%)
  starting transfers between devices  13.9 us (1%)
    psum x2, waiting for transfers between devices, per_device(): lax.psum((inner_gram(direction, image_vec), inner_gram(image_vec, image_v...  233 us
    all_to_all x1, blocking collectives, trade_out(): lax.all_to_all(buffer, ('arc', 'vec'), split_axis=0, concat_axis=0, tiled...  120 us
    all_to_all x1, blocking collectives, trade_back(): lax.all_to_all(buffer, ('arc', 'vec'), split_axis=0, concat_axis=0, tiled...  120 us
    all_to_all x1, waiting for transfers between devices, trade_out(): lax.all_to_all(buffer, ('arc', 'vec'), split_axis=0, concat_axis=0, tiled...  116 us
    all_gather x1, waiting for transfers between devices, per_device(): lax.all_gather(inner_gram(residual, residual), ('arc', 'vec'))  98.6 us
    scatter x2, local copies, waits for them, and re-layouts, per_device(): returning = jnp.zeros((device_count * slot_count, block_rows, rhs_count),...  38.8 us
    another operation x6, other arithmetic, per_device(): factor_low = jnp.linalg.cholesky(curv_gram)  25.6 us
    another operation x4, other arithmetic, per_device(): step_mat = jax.scipy.linalg.cho_solve((factor_low, True), res_gram)  22.5 us
  transfers between devices with their start and end apart: 5, of which 5 were waited for; matrix products, arithmetic and copies ran while one was open for 3% of the time, Pallas kernels for 0%

profile of v1, /device:TPU:1, one launch (start us, length us, event | category | flops | bytes accessed | tf_op | source)
XLA Modules:
  0.0 987.9 jit_solution(3203508650308277009)
XLA Ops:
  15.8 8.8 gather_fusion
  24.6 5.3 broadcast_select_fusion.1
  29.9 7.1 all-to-all-start
  37.1 116.3 %all-to-all-done = bf16[160,128,128]{2,1,0:T(8,128)(2,1)} async-done(((bf16[160,128,128]{2,1,0:T(8,128)(2,1)}), bf16[160,128,128]{2,1,0:T(8,128)(2,1)}, u32[]{:S(2)}, u32[]{:S(2)}) %all-to-all-start) | async-done | bytes 5242912 | tf_op jit(solution)/shard_map/all_to_all | solution.py:22
  153.4 5.6 gather_fusion.1
  159.0 9.2 convolution_convert_fusion.4
  168.2 7.3 convert_bitcast_fusion.1
  175.4 6.4 copy.138
  181.8 3.7 broadcast.116.clone
  185.5 19.3 %scatter_fusion = bf16[160,128,128]{2,1,0:T(8,128)(2,1)} fusion(bf16[160,128,128]{2,1,0:T(8,128)(2,1)} %broadcast.116.clone, s32[128]{0:T(128)S(1)} %fusion.35, bf16[128,128,128]{2,1,0:T(8,128)(2,1)} %bitcast.114), kind=kCustom, calls=%fused_computation.4 | custom fusion | bytes 12583424 | tf_op jit(solution)/shard_map/scatter | solution.py:86
  204.8 6.1 all-to-all-start.1
  215.1 98.6 %all-gather.3.cloned.1.call-done = f32[4096,128]{1,0:T(8,128)} async-done(((f32[128,128]{1,0:T(8,128)}), f32[4096,128]{1,0:T(8,128)}) %all-gather.3.cloned.1.call-update) | async-done | bytes 2097168 | tf_op jit(solution)/shard_map/all_gather | solution.py:62
  316.2 12.5 %cholesky.70 = f32[128,128]{1,0:T(8,128)S(1)} custom-call(f32[128,128]{1,0:T(8,128)} %fusion.19), custom_call_target="Cholesky" | custom-call | tf_op jit(solution)/shard_map/jit(cholesky)/cholesky | solution.py:108
  329.5 7.1 all-to-all-done.1
  336.6 5.4 fusion.2
  345.6 3.6 convolution_bitcast_fusion.7
  350.6 11.3 %custom-call.10 = f32[1,128,128]{1,2,0:T(8,128)} custom-call(f32[1,128,128]{2,1,0:T(8,128)} %fusion.10), custom_call_target="InvertDiagBlocksLowerTriangular" | custom-call | tf_op jit(solution)/shard_map/jit(_cho_solve)/triangular_solve | solution.py:108
  361.9 114.3 %all-reduce.6.cloned.1.call-done = (f32[128,128]{0,1:T(8,128)}, f32[128,128]{1,0:T(8,128)}) async-done(((f32[128,128]{0,1:T(8,128)}, f32[128,128]{1,0:T(8,128)}), (f32[128,128]{0,1:T(8,128)}, f32[128,128]{1,0:T(8,128)})) %all-reduce.6.cloned.1.call-update) | async-done | bytes 131088 | tf_op jit(solution)/shard_map/psum | solution.py:91
  478.7 12.5 %cholesky.59 = f32[128,128]{1,0:T(8,128)S(1)} custom-call(f32[128,128]{1,0:T(8,128)} %fusion.26), custom_call_target="Cholesky" | custom-call | tf_op jit(solution)/shard_map/jit(cholesky)/cholesky | solution.py:99
  493.2 10.6 %custom-call.9 = f32[1,128,128]{1,2,0:T(8,128)S(1)} custom-call(f32[1,128,128]{2,1,0:T(8,128)} %fusion.9), custom_call_target="InvertDiagBlocksLowerTriangular" | custom-call | tf_op jit(solution)/shard_map/jit(_cho_solve)/triangular_solve | solution.py:100
  514.0 8.9 gather_fusion.2
  525.8 119.9 %all_to_all.20 = bf16[160,128,128]{2,1,0:T(8,128)(2,1)} all-to-all(bf16[160,128,128]{2,1,0:T(8,128)(2,1)S(1)} %broadcast_select_fusion), channel_id=1, replica_groups=mesh['arc'=8,'vec'=4] {'arc','vec'}, dimensions={0} | all-to-all | bytes 10485760 | tf_op jit(solution)/shard_map/all_to_all | solution.py:22
  645.7 5.7 gather_fusion.3
  651.4 9.2 convolution_convert_fusion.1
  660.6 7.2 convert_bitcast_fusion
  667.8 6.5 copy.150
  677.9 19.5 %scatter_fusion.1 = bf16[160,128,128]{2,1,0:T(8,128)(2,1)} fusion(bf16[160,128,128]{2,1,0:T(8,128)(2,1)} %broadcast.116, s32[128]{0:T(128)} %copy-done.15, bf16[128,128,128]{2,1,0:T(8,128)(2,1)} %bitcast.113), kind=kCustom, calls=%fused_computation.5 | custom fusion | bytes 12583424 | tf_op jit(solution)/shard_map/scatter | solution.py:86
  697.4 119.8 %all_to_all.21 = bf16[160,128,128]{2,1,0:T(8,128)(2,1)S(1)} all-to-all(bf16[160,128,128]{2,1,0:T(8,128)(2,1)} %scatter_fusion.1), channel_id=1, replica_groups=mesh['arc'=8,'vec'=4] {'arc','vec'}, dimensions={0} | all-to-all | bytes 10485760 | tf_op jit(solution)/shard_map/all_to_all | solution.py:26
  827.1 118.8 %all-reduce.4.cloned.1.call-done = f32[128,128]{0,1:T(8,128)} async-done(((f32[128,128]{0,1:T(8,128)}), f32[128,128]{0,1:T(8,128)}) %all-reduce.4.cloned.1.call-update) | async-done | bytes 65552 | tf_op jit(solution)/shard_map/psum | solution.py:91
  947.7 11.7 %cholesky.81 = f32[128,128]{1,0:T(8,128)S(1)} custom-call(f32[128,128]{1,0:T(8,128)S(1)} %fusion.15), custom_call_target="Cholesky" | custom-call | tf_op jit(solution)/shard_map/jit(cholesky)/cholesky | solution.py:99
  960.8 10.0 %custom-call.11 = f32[1,128,128]{1,2,0:T(8,128)S(1)} custom-call(f32[1,128,128]{2,1,0:T(8,128)S(1)} %fusion.11), custom_call_target="InvertDiagBlocksLowerTriangular" | custom-call | tf_op jit(solution)/shard_map/jit(_cho_solve)/triangular_solve | solution.py:100
  971.3 4.7 convolution_subtract_fusion
  (96 shorter events, 60.5 us)
Async XLA Ops:
  7.2 151.8 %copy-start = (bf16[16,256,256]{2,1,0:T(8,128)(2,1)S(1)}, bf16[16,256,256]{2,1,0:T(8,128)(2,1)}, u32[]{:S(2)}) copy-start(bf16[16,256,256]{2,1,0:T(8,128)(2,1)} %param.11) | copy-start | bytes 6291460
  7.2 7.6 copy-start.1
  14.8 9.8 copy-start.14
  29.9 123.5 %all-to-all-start = ((bf16[160,128,128]{2,1,0:T(8,128)(2,1)}), bf16[160,128,128]{2,1,0:T(8,128)(2,1)}, u32[]{:S(2)}, u32[]{:S(2)}) async-start(bf16[160,128,128]{2,1,0:T(8,128)(2,1)} %broadcast_select_fusion.1), calls=%async_computation | async-start | bytes 10485760 | tf_op jit(solution)/shard_map/all_to_all | solution.py:22
  37.0 148.5 %copy-start.15 = (s32[128]{0:T(128)}, s32[128]{0:T(128)S(1)}, u32[]{:S(2)}) copy-start(s32[128]{0:T(128)S(1)} %fusion.35) | copy-start | bytes 1540
  37.1 121.9 %copy-start.16 = (s32[1024]{0:T(1024)}, s32[1024]{0:T(1024)S(1)}, u32[]{:S(2)}) copy-start(s32[1024]{0:T(1024)S(1)} %pad_clamp_fusion) | copy-start | bytes 12292
  204.8 131.8 %all-to-all-start.1 = ((bf16[160,128,128]{2,1,0:T(8,128)(2,1)}), bf16[160,128,128]{2,1,0:T(8,128)(2,1)}, u32[]{:S(2)}, u32[]{:S(2)}) async-start(bf16[160,128,128]{2,1,0:T(8,128)(2,1)} %scatter_fusion), calls=%async_computation.1 | async-start | bytes 10485760 | tf_op jit(solution)/shard_map/all_to_all | solution.py:26
  211.0 102.8 %all-gather.3.cloned.1.call-start = ((), (), s32[]{:S(2)}) async-start(), calls=%async_computation.5 | async-start | bytes 2162688 | tf_op jit(solution)/shard_map/all_gather | solution.py:62
  213.9 262.3 %all-reduce.6.cloned.1.call-start = ((), (), s32[]{:S(2)}) async-start(), calls=%async_computation.6 | async-start | bytes 262144 | tf_op jit(solution)/shard_map/psum | solution.py:91
  329.5 12.5 %copy-start.9 = (f32[20,128]{1,0:T(8,128)S(1)}, f32[20,128]{1,0:T(8,128)}, u32[]{:S(2)}) copy-start(f32[20,128]{1,0:T(8,128)} %param.10) | copy-start | bytes 30724
  342.0 3.6 copy-start.4
  349.3 596.6 %all-reduce.4.cloned.1.call-start = ((), (), s32[]{:S(2)}) async-start(), calls=%async_computation.4 | async-start | bytes 131072 | tf_op jit(solution)/shard_map/psum | solution.py:91
  503.8 0.6 copy-start.11
  505.8 4.0 copy-start.12
  507.0 3.1 copy-start.8
  507.0 3.7 copy-start.10
  509.8 4.1 copy-start.5
  697.4 119.8 %copy-start.13 = (s32[160]{0:T(256)S(1)}, s32[160]{0:T(256)}, u32[]{:S(2)}) copy-start(s32[160]{0:T(256)} %eq.60) | copy-start | bytes 1924
  817.2 4.1 copy-start.2
  820.1 1.2 copy-start.6
  971.2 4.7 copy-start.3
  971.2 4.7 copy-start.7
Sparse Core Ops, SparseCore 0:
  215.2 98.5 all-gather.2
  349.4 126.8 all-reduce.5
  824.9 120.9 all-reduce.3
